TPU v7x, 32 devices: a whole 2x2x4 slice. The times are simulated.
32 devices in a mesh: ch: 4 (over y, x), row: 8 (over z, core).
Axes of the slice: x: 2, y: 2, z: 4, core: 2. Of those that a mesh axis runs over, the one named last changes fastest.
Arguments:
- latent: bfloat16 [128, 32, 1280], P('row', None, 'ch'), may hold values from -50 to 50
- timestep: int32 [4], replicated, may hold values from 0 to 999
- norm_gain_a: float32 [1280], P('ch'), may hold values from 0.1 to 1.9
- conv_weight_a: bfloat16 [1280, 3, 3, 1280], P('ch'), may hold values from -0.0546875 to 0.0546875
- time_weight: bfloat16 [320, 1280], P(None, 'ch'), may hold values from -0.3125 to 0.3125
- norm_gain_b: float32 [1280], P('ch'), may hold values from 0.1 to 1.9
- conv_weight_b: bfloat16 [1280, 3, 3, 1280], P('ch'), may hold values from -0.0546875 to 0.0546875
- norm_gain_c: float32 [1280], P('ch'), may hold values from 0.1 to 1.9
- w_query: bfloat16 [1024, 1280], P('ch'), may hold values from -4 to 4
- w_key: bfloat16 [1024, 1280], P('ch'), may hold values from -4 to 4
- w_value: bfloat16 [1024, 1280], P('ch'), may hold values from -0.3125 to 0.3125
- w_out: bfloat16 [1280, 1024], P('ch'), may hold values from -0.1875 to 0.1875
Outputs:
- result: bfloat16 [128, 32, 1280], P('row', None, 'ch')
All inputs are finite; a program needn't handle non-finite values.
Results may differ from a plain program's by a relative error of at most 0.017.
Values may be sent and summed in bfloat16 or wider, within the bound.
A program may use at most 64 MiB of HBM per device.

v0:
```python
import math
import jax
import jax.numpy as jnp
from jax import lax
from jax.sharding import PartitionSpec as P

C = 1280
GROUPS = 32
HEAD_DIM = 64
TDIM = 320
H = 32
eps_value = 1e-06


def swapped(value, axis, stride):
    mask = 2**stride
    pairs = [(source, source ^ mask) for source in range(lax.axis_size(axis))]
    return lax.ppermute(value, axis, pairs)


def right_product(left, weight):
    return lax.dot_general(
        left, weight, (((1,), (1,)), ((), ())), preferred_element_type=jnp.float32
    )


def conv_taps(padded, weight):
    outcome = lax.conv_general_dilated(
        padded[None],
        weight,
        (1, 1),
        "VALID",
        dimension_numbers=("NHWC", "OHWI", "NHWC"),
        preferred_element_type=jnp.float32,
    )
    return outcome[0]


def pad_columns(field):
    return jnp.pad(field, ((0, 0), (1, 1), (0, 0)))


def body(
    latent,
    timestep,
    norm_gain_a,
    conv_weight_a,
    time_weight,
    norm_gain_b,
    conv_weight_b,
    norm_gain_c,
    w_query,
    w_key,
    w_value,
    w_out,
):
    rows, width, local_ch = latent.shape
    span = H // rows
    place = lax.axis_index("row")
    within = place % span
    image_id = place // span
    group_width = C // GROUPS
    local_groups = local_ch // group_width
    members = float(H * width * group_width)
    tokens = rows * width

    def group_norm(value, gain):
        flat = value.reshape(tokens, local_groups, group_width)
        stats = jnp.stack([jnp.sum(flat, axis=(0, 2)), jnp.sum(flat * flat, axis=(0, 2))])
        stats = stats + swapped(stats, "row", 0)
        mean = stats[0] / members
        spread = stats[1] / members - mean * mean
        scaled = (flat - mean[None, :, None]) * lax.rsqrt(spread + eps_value)[None, :, None]
        return scaled.reshape(rows, width, local_ch) * gain

    upper_half = within == 0

    def facing_row(field):
        return jnp.where(upper_half, field[-1:], field[:1])

    def attach_rim(field, partner):
        empty_row = jnp.zeros_like(partner)
        above = jnp.where(upper_half, empty_row, partner)
        below = jnp.where(upper_half, partner, empty_row)
        return jnp.concatenate([above, field, below], axis=0)

    def convolve(active, weight):
        full = lax.all_gather(active, "ch", axis=2, tiled=True)
        partner = swapped(facing_row(full), "row", 0)
        rimmed = attach_rim(full, partner)
        result_conv = conv_taps(pad_columns(rimmed), weight)
        return result_conv

    image_ids = jnp.arange(timestep.shape[0])
    step_value = jnp.sum(jnp.where(image_ids == image_id, timestep, 0)).astype(jnp.float32)
    half = TDIM // 2
    freqs = jnp.exp(-math.log(10000.0) * jnp.arange(half, dtype=jnp.float32) / half)
    angles = step_value * freqs
    sinus = jnp.concatenate([jnp.cos(angles), jnp.sin(angles)])[None, :].astype(jnp.bfloat16)
    time_add = jax.nn.silu(jnp.dot(sinus, time_weight, preferred_element_type=jnp.float32))
    source = latent.astype(jnp.float32)
    active_a = jax.nn.silu(group_norm(source, norm_gain_a)).astype(jnp.bfloat16)
    hidden_a = convolve(active_a, conv_weight_a) + time_add[None]
    active_b = jax.nn.silu(group_norm(hidden_a, norm_gain_b)).astype(jnp.bfloat16)
    hidden_b = source + convolve(active_b, conv_weight_b)
    normed = group_norm(hidden_b, norm_gain_c).astype(jnp.bfloat16).reshape(tokens, local_ch)
    inner = w_query.shape[0]
    projections = jnp.concatenate([w_query, w_key, w_value], axis=0)
    weight_cols = projections
    mixed = right_product(lax.all_gather(normed, "ch", axis=1, tiled=True), weight_cols)
    query = mixed[:, :inner].astype(jnp.bfloat16)
    keyed = mixed[:, inner : 2 * inner].astype(jnp.bfloat16)
    valued = mixed[:, 2 * inner :].astype(jnp.bfloat16)
    key_value = jnp.stack([keyed, valued])
    key_value = jnp.concatenate([key_value, swapped(key_value, "row", 0)], axis=1)
    local_heads = inner // HEAD_DIM
    query_heads = query.reshape(tokens, local_heads, HEAD_DIM)
    key_heads = key_value[0].reshape(-1, local_heads, HEAD_DIM)
    value_heads = key_value[1].reshape(-1, local_heads, HEAD_DIM)
    scores = jnp.einsum(
        "qhd,khd->hqk", query_heads, key_heads, preferred_element_type=jnp.float32
    ) * (1.0 / math.sqrt(HEAD_DIM))
    highest = jnp.max(scores, axis=-1, keepdims=True)
    raised = jnp.exp(scores - highest)
    weights = (raised / jnp.sum(raised, axis=-1, keepdims=True)).astype(jnp.bfloat16)
    heads_out = jnp.einsum("hqk,khd->qhd", weights, value_heads, preferred_element_type=jnp.float32)
    heads_out = heads_out.astype(jnp.bfloat16).reshape(tokens, inner)
    weight_cols = w_out
    projected = right_product(lax.all_gather(heads_out, "ch", axis=1, tiled=True), weight_cols)
    total = hidden_b.reshape(tokens, local_ch) + projected
    return total.reshape(rows, width, local_ch).astype(jnp.bfloat16)


def solution(mesh):
    return jax.shard_map(
        body,
        mesh=mesh,
        in_specs=(
            P("row", None, "ch"),
            P(),
            P("ch"),
            P("ch", None, None, None),
            P(None, "ch"),
            P("ch"),
            P("ch", None, None, None),
            P("ch"),
            P("ch", None),
            P("ch", None),
            P("ch", None),
            P("ch", None),
        ),
        out_specs=P("row", None, "ch"),
        check_vma=False,
    )
```

profile of v0, /device:TPU:0, one launch (start us, length us, event | category | flops | bytes accessed | tf_op | source)
XLA Modules:
  0.0 277.8 jit_solution(7291214916432832792)
XLA Ops:
  6.5 1.3 convert_reduce_fusion
  8.2 0.6 collective-permute-start
  8.8 0.8 collective-permute-done
  9.9 1.3 fusion.55
  11.2 1.8 copy.96
  13.1 0.6 fusion.60
  14.6 0.2 convolution_reduce_fusion
  14.7 62.4 %all-gather.5.cloned.1.call-done = bf16[16,32,1280]{1,0,2:T(8,128)(2,1)} async-done(((bf16[16,32,320]{1,0,2:T(8,128)(2,1)}), bf16[16,32,1280]{1,0,2:T(8,128)(2,1)}) %all-gather.5.cloned.1.call-update) | async-done | bytes 1310736 | tf_op jit(solution)/shard_map/all_gather | solution.py:88
  77.1 3.0 %broadcast_select_fusion.5 = bf16[1,32,1280]{1,0,2:T(2,128)(2,1)S(1)} fusion(pred[]{:T(512)S(6)} %eq.11, bf16[16,32,1280]{1,0,2:T(8,128)(2,1)} %all-gather.5.cloned.1.call-done), kind=kLoop, calls=%fused_computation.48 | loop fusion | flops 40960 | bytes 245761 | tf_op jit(solution)/shard_map/jit(_where)/select_n | solution.py:79
  80.1 0.4 copy.97
  80.6 6.0 %copy.101 = bf16[16,32,1280]{2,1,0:T(8,128)(2,1)S(1)} copy(bf16[16,32,1280]{1,0,2:T(8,128)(2,1)} %all-gather.5.cloned.1.call-done) | data formatting | bytes 2621440 | tf_op jit(solution)/shard_map/all_gather | solution.py:88
  86.6 0.5 copy.98
  87.1 1.9 broadcast_select_fusion.4
  89.0 1.3 copy.100
  90.2 0.4 copy.102
  90.6 0.6 fusion.30
  91.3 0.3 copy.126
  91.6 0.2 pad.9.clone
  91.8 0.3 copy.105
  92.1 0.2 slice.69
  92.3 1.1 slice-done
  93.5 1.1 slice-done.1
  94.5 7.8 %select_reduce_fusion.1 = (f32[320]{0:T(512)S(1)}, f32[320]{0:T(512)S(1)}, f32[16,8,5,320]{3,1,2,0:T(8,128)S(1)}) fusion(f32[320]{0:T(512)S(1)} %divide_multiply_fusion, pred[8,5]{0,1:T(8,128)(4,1)S(1)} %copy-done.8, bf16[320,3,3,1280]{3,0,2,1:T(8,128)(2,1)S(1)} %bitcast.121, bf16[18,1,7,2,1280]{4,2,3,0,1:T(8,128)(2,1)S(1)} %slice.69, ...), kind=kOutput, calls=%fused_computation.59 | convolution fusion | flops 4727766016 | bytes 10684200 | tf_op jit(solution)/shard_map/conv_general_dilated | solution.py:28
  102.7 0.1 reduce_sum.126
  102.8 0.6 collective-permute-start.2
  103.3 0.2 copy.106
  103.5 0.6 collective-permute-done.2
  104.5 0.3 multiply_convert_fusion.1
  104.8 2.0 copy.107
  106.8 61.4 %all-gather.7.cloned.1.call-done = bf16[16,32,1280]{1,0,2:T(8,128)(2,1)} async-done(((bf16[16,32,320]{1,0,2:T(8,128)(2,1)}), bf16[16,32,1280]{1,0,2:T(8,128)(2,1)}) %all-gather.7.cloned.1.call-update) | async-done | bytes 1310736 | tf_op jit(solution)/shard_map/all_gather | solution.py:88
  168.2 3.0 %broadcast_select_fusion.2 = bf16[1,32,1280]{1,0,2:T(2,128)(2,1)S(1)} fusion(pred[]{:T(512)S(6)} %eq.11, bf16[16,32,1280]{1,0,2:T(8,128)(2,1)} %all-gather.7.cloned.1.call-done), kind=kLoop, calls=%fused_computation.45 | loop fusion | flops 40960 | bytes 245761 | tf_op jit(solution)/shard_map/jit(_where)/select_n | solution.py:79
  171.3 0.4 copy.108
  171.7 6.0 %copy.112 = bf16[16,32,1280]{2,1,0:T(8,128)(2,1)S(1)} copy(bf16[16,32,1280]{1,0,2:T(8,128)(2,1)} %all-gather.7.cloned.1.call-done) | data formatting | bytes 2621440 | tf_op jit(solution)/shard_map/all_gather | solution.py:88
  177.7 0.5 copy.109
  178.2 1.9 broadcast_select_fusion.1
  180.1 1.3 copy.111
  181.4 0.4 copy.113
  181.7 0.6 fusion.29
  182.4 0.3 copy.127
  182.7 0.2 pad.11.clone
  182.9 0.3 copy.116
  183.2 0.2 slice.73
  183.4 1.1 slice-done.2
  184.6 1.1 slice-done.3
  185.6 7.8 %fusion.35 = f32[16,8,5,320]{3,1,2,0:T(8,128)S(1)} fusion(bf16[320,3,3,1280]{3,0,2,1:T(8,128)(2,1)S(1)} %bitcast.123, bf16[18,1,7,2,1280]{4,2,3,0,1:T(8,128)(2,1)S(1)} %slice.73, bf16[18,1,8,5,1280]{4,2,3,0,1:T(8,128)(2,1)S(1)} %copy.116, pred[8,5]{0,1:T(8,128)(4,1)S(1)} %copy-done.8), kind=kOutput, calls=%fused_computation.49 | convolution fusion | flops 4726538240 | bytes 10680360 | tf_op jit(solution)/shard_map/conv_general_dilated | solution.py:28
  193.4 0.2 copy.117
  193.7 0.2 fusion.78
  194.1 0.1 reduce_sum.132
  194.3 0.6 collective-permute-start.4
  194.8 0.8 collective-permute-done.4
  196.2 0.9 copy.120
  197.2 28.8 %all-gather.9.cloned.1.call-done = bf16[512,1280]{0,1:T(8,128)(2,1)} async-done(((bf16[512,320]{0,1:T(8,128)(2,1)}), bf16[512,1280]{0,1:T(8,128)(2,1)}) %all-gather.9.cloned.1.call-update) | async-done | bytes 1310736 | tf_op jit(solution)/shard_map/all_gather | solution.py:110
  225.9 2.7 fusion.32
  228.8 0.1 copy.122
  229.0 1.7 collective-permute-done.5
  230.9 0.2 copy.123
  231.1 0.2 copy.121
  231.3 5.0 %fusion.81 = (f32[4,512]{1,0:T(4,128)S(1)}, f32[4,512,1024]{2,1,0:T(8,128)}) fusion(bf16[512,4,64]{0,2,1:T(8,128)(2,1)S(1)} %bitcast.106, bf16[1024,4,64]{0,2,1:T(8,128)(2,1)S(1)} %bitcast.104), kind=kOutput, calls=%fused_computation.118 | convolution fusion | flops 274727936 | bytes 9183232 | tf_op jit(solution)/shard_map/sub | solution.py:124
  236.4 5.5 %fusion.44 = bf16[4,64,512]{2,1,0:T(8,128)(2,1)} fusion(bf16[1024,4,64]{0,2,1:T(8,128)(2,1)S(1)} %bitcast.105, f32[4,512,1024]{2,1,0:T(8,128)} %get-tuple-element.23, f32[4,512]{1,0:T(4,128)S(1)} %get-tuple-element.22), kind=kOutput, calls=%fused_computation.55 | convolution fusion | flops 272760832 | bytes 9183232 | tf_op jit(solution)/shard_map/hqk,khd->qhd/dot_general | solution.py:126
  241.9 0.3 copy.118
  242.2 0.2 copy.124
  242.5 26.1 %all-gather.11.cloned.1.call-done = bf16[512,1024]{0,1:T(8,128)(2,1)} async-done(((bf16[512,256]{0,1:T(8,128)(2,1)}), bf16[512,1024]{0,1:T(8,128)(2,1)}) %all-gather.11.cloned.1.call-update) | async-done | bytes 1048592 | tf_op jit(solution)/shard_map/all_gather | solution.py:129
  268.6 1.7 fusion.43
  270.3 0.9 copy.125
  (81 shorter events, 3.0 us)
Async XLA Ops:
  6.5 262.1 %copy-start = (bf16[320,1024]{1,0:T(8,128)(2,1)S(1)}, bf16[320,1024]{1,0:T(8,128)(2,1)}, u32[]{:S(2)}) copy-start(bf16[320,1024]{1,0:T(8,128)(2,1)} %param.23) | copy-start | bytes 1966084
  6.5 6.6 %copy-start.7 = (s32[4]{0:T(128)S(1)}, s32[4]{0:T(128)}, u32[]{:S(2)}) copy-start(s32[4]{0:T(128)} %param.13) | copy-start | bytes 52
  6.5 8.0 %copy-start.2 = (bf16[320,320]{1,0:T(8,128)(2,1)S(1)}, bf16[320,320]{1,0:T(8,128)(2,1)}, u32[]{:S(2)}) copy-start(bf16[320,320]{1,0:T(8,128)(2,1)} %param.16) | copy-start | bytes 614404
  6.5 70.5 %all-gather.5.cloned.1.call-start = ((), (), s32[]{:S(2)}) async-start(), calls=%async_computation | async-start | bytes 6553600 | tf_op jit(solution)/shard_map/all_gather | solution.py:88
  8.2 1.4 collective-permute-start
  13.0 155.2 %all-gather.7.cloned.1.call-start = ((), (), s32[]{:S(2)}) async-start(), calls=%async_computation.1 | async-start | bytes 6553600 | tf_op jit(solution)/shard_map/all_gather | solution.py:88
  80.5 6.1 %collective-permute-start.1 = (bf16[1,32,1280]{2,1,0:T(8,128)(2,1)S(1)}, bf16[1,32,1280]{2,1,0:T(8,128)(2,1)S(1)}, u32[]{:S(2)}, u32[]{:S(2)}) collective-permute-start(bf16[1,32,1280]{2,1,0:T(8,128)(2,1)S(1)} %copy.97), channel_id=1, source_target_pairs={{0,1},{1,0},{2,3},{3,2},{4,5},{5,4},{6,7},{7,6},{8,9},{9,8},{10,11... | collective-permute-start | bytes 245768 | tf_op jit(solution)/shard_map/ppermute | solution.py:18
  91.3 2.2 slice-start
  91.6 2.9 %slice-start.1 = ((s8[7372800]{0:T(1024)(128)(4,1)}), s8[3178496]{0:T(1024)(128)(4,1)S(1)}, s32[]{:S(2)}) async-start(s8[7372800]{0:T(1024)(128)(4,1)} %bitcast.120), calls=%async_computation.5 | async-start | bytes 6356992
  91.8 2.7 copy-start.8
  94.5 10.0 %copy-start.3 = (f32[320]{0:T(512)S(1)}, f32[320]{0:T(512)}, u32[]{:S(2)}) copy-start(f32[320]{0:T(512)} %param.17) | copy-start | bytes 3844
  102.8 1.4 collective-permute-start.2
  106.8 119.2 %all-gather.9.cloned.1.call-start = ((), (), s32[]{:S(2)}) async-start(), calls=%async_computation.2 | async-start | bytes 1638400 | tf_op jit(solution)/shard_map/all_gather | solution.py:110
  171.6 6.1 %collective-permute-start.3 = (bf16[1,32,1280]{2,1,0:T(8,128)(2,1)S(1)}, bf16[1,32,1280]{2,1,0:T(8,128)(2,1)S(1)}, u32[]{:S(2)}, u32[]{:S(2)}) collective-permute-start(bf16[1,32,1280]{2,1,0:T(8,128)(2,1)S(1)} %copy.108), channel_id=1, source_target_pairs={{0,1},{1,0},{2,3},{3,2},{4,5},{5,4},{6,7},{7,6},{8,9},{9,8},{10,11... | collective-permute-start | bytes 245768 | tf_op jit(solution)/shard_map/ppermute | solution.py:18
  182.4 2.2 slice-start.2
  182.7 2.9 %slice-start.3 = ((s8[7372800]{0:T(1024)(128)(4,1)}), s8[3178496]{0:T(1024)(128)(4,1)S(1)}, s32[]{:S(2)}) async-start(s8[7372800]{0:T(1024)(128)(4,1)} %bitcast.122), calls=%async_computation.7 | async-start | bytes 6356992
  185.6 8.0 %copy-start.1 = (bf16[16,32,320]{2,1,0:T(8,128)(2,1)S(1)}, bf16[16,32,320]{2,1,0:T(8,128)(2,1)}, u32[]{:S(2)}) copy-start(bf16[16,32,320]{2,1,0:T(8,128)(2,1)} %param.12) | copy-start | bytes 983044
  193.4 2.6 copy-start.4
  193.6 32.3 %copy-start.5 = (bf16[256,1280]{1,0:T(8,128)(2,1)S(1)}, bf16[256,1280]{1,0:T(8,128)(2,1)}, u32[]{:S(2)}) copy-start(bf16[256,1280]{1,0:T(8,128)(2,1)} %param.22) | copy-start | bytes 1966084
  193.6 32.3 %copy-start.6 = (bf16[256,1280]{1,0:T(8,128)(2,1)S(1)}, bf16[256,1280]{1,0:T(8,128)(2,1)}, u32[]{:S(2)}) copy-start(bf16[256,1280]{1,0:T(8,128)(2,1)} %param.21) | copy-start | bytes 1966084
  194.3 1.4 collective-permute-start.4
  197.1 71.5 %all-gather.11.cloned.1.call-start = ((), (), s32[]{:S(2)}) async-start(), calls=%async_computation.3 | async-start | bytes 1310720 | tf_op jit(solution)/shard_map/all_gather | solution.py:129
  228.8 2.0 collective-permute-start.5
Sparse Core Ops, SparseCore 0:
  13.2 63.8 all-gather.4
  106.9 61.2 all-gather.6
  197.2 28.6 all-gather.8
  242.1 26.4 all-gather.10
where the time goes:
time: 278 us
  waiting for transfers between devices  183 us (66%)
  local copies, waits for them, and re-layouts  32 us (12%)
  matrix products  30.8 us (11%)
  other arithmetic  15.9 us (6%)
  between operations  14.3 us (5%)
    all_gather x2, waiting for transfers between devices, convolve(): full = lax.all_gather(active, 'ch', axis=2, tiled=True)  124 us
    all_gather x1, waiting for transfers between devices, body(): lax.all_gather(normed, 'ch', axis=1, tiled=True)  28.8 us
    all_gather x1, waiting for transfers between devices, body(): lax.all_gather(heads_out, 'ch', axis=1, tiled=True)  26.1 us
    conv_general_dilated x2, matrix products, conv_taps(): lax.conv_general_dilated(padded[None], weight, (1, 1), 'VALID', dimension...  15.6 us
    all_gather x2, local copies, waits for them, and re-layouts, convolve(): full = lax.all_gather(active, 'ch', axis=2, tiled=True)  12 us
    select_n x2, other arithmetic, facing_row(): return jnp.where(upper_half, field[-1:], field[:1])  6.06 us
  transfers between devices with their start and end apart: 10, of which 8 were waited for; matrix products, arithmetic and copies ran while one was open for 5% of the time, Pallas kernels for 0%

commit v1 on v0

--- a/solution.py
+++ b/solution.py
@@ -10,6 +10,9 @@
 TDIM = 320
 H = 32
 eps_value = 1e-06
+search_the_heads = lambda local_block: jnp.concatenate(
+    lax.all_gather(local_block, axis_name="ch"), axis=1
+)
 
 
 def swapped(value, axis, stride):
@@ -126,7 +129,7 @@
     heads_out = jnp.einsum("hqk,khd->qhd", weights, value_heads, preferred_element_type=jnp.float32)
     heads_out = heads_out.astype(jnp.bfloat16).reshape(tokens, inner)
     weight_cols = w_out
-    projected = right_product(lax.all_gather(heads_out, "ch", axis=1, tiled=True), weight_cols)
+    projected = right_product(search_the_heads(heads_out), weight_cols)
     total = hidden_b.reshape(tokens, local_ch) + projected
     return total.reshape(rows, width, local_ch).astype(jnp.bfloat16)
 

time: 278 us -> 279 us (level)
  no operation moved by 1% of the time
where the time goes in v1:
time: 279 us; the launch traced here: 278 us
  waiting for transfers between devices  183 us (66%)
  local copies, waits for them, and re-layouts  34.4 us (12%)
  matrix products  28.8 us (10%)
  other arithmetic  15.9 us (6%)
  between operations  14.3 us (5%)
    all_gather x2, waiting for transfers between devices, convolve(): full = lax.all_gather(active, 'ch', axis=2, tiled=True)  124 us
    all_gather x1, waiting for transfers between devices, body(): lax.all_gather(normed, 'ch', axis=1, tiled=True)  28.8 us
    all_gather x1, waiting for transfers between devices, lax.all_gather(local_block, axis_name='ch')  26.1 us
    conv_general_dilated x2, matrix products, conv_taps(): lax.conv_general_dilated(padded[None], weight, (1, 1), 'VALID', dimension...  15.6 us
    all_gather x2, local copies, waits for them, and re-layouts, convolve(): full = lax.all_gather(active, 'ch', axis=2, tiled=True)  12 us
    select_n x2, other arithmetic, facing_row(): return jnp.where(upper_half, field[-1:], field[:1])  6.06 us
  transfers between devices with their start and end apart: 10, of which 8 were waited for; matrix products, arithmetic and copies ran while one was open for 5% of the time, Pallas kernels for 0%

profile of v1, /device:TPU:0, one launch (start us, length us, event | category | flops | bytes accessed | tf_op | source)
XLA Modules:
  0.0 278.2 jit_solution(15692118238806772615)
XLA Ops:
  6.5 1.3 convert_reduce_fusion
  8.2 0.6 collective-permute-start
  8.8 0.8 collective-permute-done
  9.9 1.3 fusion.55
  11.2 1.8 copy.120
  13.1 0.6 fusion.60
  14.6 0.2 convolution_reduce_fusion
  14.7 62.4 %all-gather.5.cloned.1.call-done = bf16[16,32,1280]{1,0,2:T(8,128)(2,1)} async-done(((bf16[16,32,320]{1,0,2:T(8,128)(2,1)}), bf16[16,32,1280]{1,0,2:T(8,128)(2,1)}) %all-gather.5.cloned.1.call-update) | async-done | bytes 1310736 | tf_op jit(solution)/shard_map/all_gather | solution.py:91
  77.1 3.0 %broadcast_select_fusion.5 = bf16[1,32,1280]{1,0,2:T(2,128)(2,1)S(1)} fusion(pred[]{:T(512)S(6)} %eq.11, bf16[16,32,1280]{1,0,2:T(8,128)(2,1)} %all-gather.5.cloned.1.call-done), kind=kLoop, calls=%fused_computation.48 | loop fusion | flops 40960 | bytes 245761 | tf_op jit(solution)/shard_map/jit(_where)/select_n | solution.py:82
  80.1 0.4 copy.121
  80.6 6.0 %copy.125 = bf16[16,32,1280]{2,1,0:T(8,128)(2,1)S(1)} copy(bf16[16,32,1280]{1,0,2:T(8,128)(2,1)} %all-gather.5.cloned.1.call-done) | data formatting | bytes 2621440 | tf_op jit(solution)/shard_map/all_gather | solution.py:91
  86.6 0.5 copy.122
  87.1 1.9 broadcast_select_fusion.4
  89.0 1.3 copy.124
  90.2 0.4 copy.126
  90.6 0.6 fusion.30
  91.3 0.3 copy.152
  91.6 0.2 pad.9.clone
  91.8 0.3 copy.129
  92.1 0.2 slice.69
  92.3 1.1 slice-done
  93.5 1.1 slice-done.1
  94.5 7.8 %select_reduce_fusion.1 = (f32[320]{0:T(512)S(1)}, f32[320]{0:T(512)S(1)}, f32[16,8,5,320]{3,1,2,0:T(8,128)S(1)}) fusion(f32[320]{0:T(512)S(1)} %divide_multiply_fusion, pred[8,5]{0,1:T(8,128)(4,1)S(1)} %copy-done.8, bf16[320,3,3,1280]{3,0,2,1:T(8,128)(2,1)S(1)} %bitcast.125, bf16[18,1,7,2,1280]{4,2,3,0,1:T(8,128)(2,1)S(1)} %slice.69, ...), kind=kOutput, calls=%fused_computation.59 | convolution fusion | flops 4727766016 | bytes 10684200 | tf_op jit(solution)/shard_map/conv_general_dilated | solution.py:31
  102.8 0.6 collective-permute-start.2
  103.3 0.2 copy.130
  103.5 0.6 collective-permute-done.2
  104.5 0.3 multiply_convert_fusion.1
  104.8 2.0 copy.131
  106.8 61.4 %all-gather.7.cloned.1.call-done = bf16[16,32,1280]{1,0,2:T(8,128)(2,1)} async-done(((bf16[16,32,320]{1,0,2:T(8,128)(2,1)}), bf16[16,32,1280]{1,0,2:T(8,128)(2,1)}) %all-gather.7.cloned.1.call-update) | async-done | bytes 1310736 | tf_op jit(solution)/shard_map/all_gather | solution.py:91
  168.2 3.0 %broadcast_select_fusion.2 = bf16[1,32,1280]{1,0,2:T(2,128)(2,1)S(1)} fusion(pred[]{:T(512)S(6)} %eq.11, bf16[16,32,1280]{1,0,2:T(8,128)(2,1)} %all-gather.7.cloned.1.call-done), kind=kLoop, calls=%fused_computation.45 | loop fusion | flops 40960 | bytes 245761 | tf_op jit(solution)/shard_map/jit(_where)/select_n | solution.py:82
  171.3 0.4 copy.132
  171.7 6.0 %copy.136 = bf16[16,32,1280]{2,1,0:T(8,128)(2,1)S(1)} copy(bf16[16,32,1280]{1,0,2:T(8,128)(2,1)} %all-gather.7.cloned.1.call-done) | data formatting | bytes 2621440 | tf_op jit(solution)/shard_map/all_gather | solution.py:91
  177.7 0.5 copy.133
  178.2 1.9 broadcast_select_fusion.1
  180.1 1.3 copy.135
  181.4 0.4 copy.137
  181.7 0.6 fusion.29
  182.4 0.3 copy.153
  182.7 0.2 pad.11.clone
  182.9 0.3 copy.140
  183.2 0.2 slice.73
  183.4 1.1 slice-done.2
  184.6 1.1 slice-done.3
  185.6 7.8 %fusion.35 = f32[16,8,5,320]{3,1,2,0:T(8,128)S(1)} fusion(bf16[320,3,3,1280]{3,0,2,1:T(8,128)(2,1)S(1)} %bitcast.127, bf16[18,1,7,2,1280]{4,2,3,0,1:T(8,128)(2,1)S(1)} %slice.73, bf16[18,1,8,5,1280]{4,2,3,0,1:T(8,128)(2,1)S(1)} %copy.140, pred[8,5]{0,1:T(8,128)(4,1)S(1)} %copy-done.8), kind=kOutput, calls=%fused_computation.49 | convolution fusion | flops 4726538240 | bytes 10680360 | tf_op jit(solution)/shard_map/conv_general_dilated | solution.py:31
  193.4 0.2 copy.141
  193.7 0.2 fusion.78
  194.3 0.6 collective-permute-start.4
  194.8 0.8 collective-permute-done.4
  196.2 0.9 copy.144
  197.2 28.8 %all-gather.9.cloned.1.call-done = bf16[512,1280]{0,1:T(8,128)(2,1)} async-done(((bf16[512,320]{0,1:T(8,128)(2,1)}), bf16[512,1280]{0,1:T(8,128)(2,1)}) %all-gather.9.cloned.1.call-update) | async-done | bytes 1310736 | tf_op jit(solution)/shard_map/all_gather | solution.py:113
  225.9 2.7 fusion.32
  228.8 0.1 copy.146
  229.0 1.7 collective-permute-done.5
  230.9 0.2 copy.147
  231.1 0.2 copy.145
  231.3 5.0 %fusion.81 = (f32[4,512]{1,0:T(4,128)S(1)}, f32[4,512,1024]{2,1,0:T(8,128)}) fusion(bf16[512,4,64]{0,2,1:T(8,128)(2,1)S(1)} %bitcast.110, bf16[1024,4,64]{0,2,1:T(8,128)(2,1)S(1)} %bitcast.108), kind=kOutput, calls=%fused_computation.118 | convolution fusion | flops 274727936 | bytes 9183232 | tf_op jit(solution)/shard_map/sub | solution.py:127
  236.4 4.8 %fusion.44 = bf16[4,64,512]{2,1,0:T(8,128)(2,1)S(1)} fusion(bf16[1024,4,64]{0,2,1:T(8,128)(2,1)S(1)} %bitcast.109, f32[4,512,1024]{2,1,0:T(8,128)} %get-tuple-element.23, f32[4,512]{1,0:T(4,128)S(1)} %get-tuple-element.22), kind=kOutput, calls=%fused_computation.55 | convolution fusion | flops 272760832 | bytes 9183232 | tf_op jit(solution)/shard_map/hqk,khd->qhd/dot_general | solution.py:129
  241.2 0.8 copy.148
  242.1 0.3 copy.142
  242.3 0.2 copy.150
  242.6 26.1 %all-gather.11.cloned.1.call-done = bf16[4,512,256]{2,1,0:T(8,128)(2,1)} async-done(((bf16[1,512,256]{2,1,0:T(8,128)(2,1)}), bf16[4,512,256]{2,1,0:T(8,128)(2,1)}) %all-gather.11.cloned.1.call-update) | async-done | bytes 1048592 | tf_op jit(solution)/shard_map/all_gather | solution.py:14
  268.7 1.5 copy.149
  270.2 0.5 fusion.43
  270.7 0.9 copy.151
  (83 shorter events, 3.2 us)
Async XLA Ops:
  6.5 263.7 %copy-start = (bf16[320,1024]{1,0:T(8,128)(2,1)S(1)}, bf16[320,1024]{1,0:T(8,128)(2,1)}, u32[]{:S(2)}) copy-start(bf16[320,1024]{1,0:T(8,128)(2,1)} %param.23) | copy-start | bytes 1966084
  6.5 6.6 %copy-start.7 = (s32[4]{0:T(128)S(1)}, s32[4]{0:T(128)}, u32[]{:S(2)}) copy-start(s32[4]{0:T(128)} %param.13) | copy-start | bytes 52
  6.5 8.0 %copy-start.2 = (bf16[320,320]{1,0:T(8,128)(2,1)S(1)}, bf16[320,320]{1,0:T(8,128)(2,1)}, u32[]{:S(2)}) copy-start(bf16[320,320]{1,0:T(8,128)(2,1)} %param.16) | copy-start | bytes 614404
  6.5 70.5 %all-gather.5.cloned.1.call-start = ((), (), s32[]{:S(2)}) async-start(), calls=%async_computation | async-start | bytes 6553600 | tf_op jit(solution)/shard_map/all_gather | solution.py:91
  8.2 1.4 collective-permute-start
  13.0 155.2 %all-gather.7.cloned.1.call-start = ((), (), s32[]{:S(2)}) async-start(), calls=%async_computation.1 | async-start | bytes 6553600 | tf_op jit(solution)/shard_map/all_gather | solution.py:91
  80.5 6.1 %collective-permute-start.1 = (bf16[1,32,1280]{2,1,0:T(8,128)(2,1)S(1)}, bf16[1,32,1280]{2,1,0:T(8,128)(2,1)S(1)}, u32[]{:S(2)}, u32[]{:S(2)}) collective-permute-start(bf16[1,32,1280]{2,1,0:T(8,128)(2,1)S(1)} %copy.121), channel_id=1, source_target_pairs={{0,1},{1,0},{2,3},{3,2},{4,5},{5,4},{6,7},{7,6},{8,9},{9,8},{10,11... | collective-permute-start | bytes 245768 | tf_op jit(solution)/shard_map/ppermute | solution.py:21
  91.3 2.2 slice-start
  91.6 2.9 %slice-start.1 = ((s8[7372800]{0:T(1024)(128)(4,1)}), s8[3178496]{0:T(1024)(128)(4,1)S(1)}, s32[]{:S(2)}) async-start(s8[7372800]{0:T(1024)(128)(4,1)} %bitcast.124), calls=%async_computation.5 | async-start | bytes 6356992
  91.8 2.7 copy-start.8
  94.5 10.0 %copy-start.3 = (f32[320]{0:T(512)S(1)}, f32[320]{0:T(512)}, u32[]{:S(2)}) copy-start(f32[320]{0:T(512)} %param.17) | copy-start | bytes 3844
  102.8 1.4 collective-permute-start.2
  106.8 119.2 %all-gather.9.cloned.1.call-start = ((), (), s32[]{:S(2)}) async-start(), calls=%async_computation.2 | async-start | bytes 1638400 | tf_op jit(solution)/shard_map/all_gather | solution.py:113
  171.6 6.1 %collective-permute-start.3 = (bf16[1,32,1280]{2,1,0:T(8,128)(2,1)S(1)}, bf16[1,32,1280]{2,1,0:T(8,128)(2,1)S(1)}, u32[]{:S(2)}, u32[]{:S(2)}) collective-permute-start(bf16[1,32,1280]{2,1,0:T(8,128)(2,1)S(1)} %copy.132), channel_id=1, source_target_pairs={{0,1},{1,0},{2,3},{3,2},{4,5},{5,4},{6,7},{7,6},{8,9},{9,8},{10,11... | collective-permute-start | bytes 245768 | tf_op jit(solution)/shard_map/ppermute | solution.py:21
  182.4 2.2 slice-start.2
  182.7 2.9 %slice-start.3 = ((s8[7372800]{0:T(1024)(128)(4,1)}), s8[3178496]{0:T(1024)(128)(4,1)S(1)}, s32[]{:S(2)}) async-start(s8[7372800]{0:T(1024)(128)(4,1)} %bitcast.126), calls=%async_computation.7 | async-start | bytes 6356992
  185.6 8.0 %copy-start.1 = (bf16[16,32,320]{2,1,0:T(8,128)(2,1)S(1)}, bf16[16,32,320]{2,1,0:T(8,128)(2,1)}, u32[]{:S(2)}) copy-start(bf16[16,32,320]{2,1,0:T(8,128)(2,1)} %param.12) | copy-start | bytes 983044
  193.4 2.6 copy-start.4
  193.6 32.3 %copy-start.5 = (bf16[256,1280]{1,0:T(8,128)(2,1)S(1)}, bf16[256,1280]{1,0:T(8,128)(2,1)}, u32[]{:S(2)}) copy-start(bf16[256,1280]{1,0:T(8,128)(2,1)} %param.22) | copy-start | bytes 1966084
  193.6 32.3 %copy-start.6 = (bf16[256,1280]{1,0:T(8,128)(2,1)S(1)}, bf16[256,1280]{1,0:T(8,128)(2,1)}, u32[]{:S(2)}) copy-start(bf16[256,1280]{1,0:T(8,128)(2,1)} %param.21) | copy-start | bytes 1966084
  194.3 1.4 collective-permute-start.4
  197.1 71.6 %all-gather.11.cloned.1.call-start = ((), (), s32[]{:S(2)}) async-start(), calls=%async_computation.3 | async-start | bytes 1310720 | tf_op jit(solution)/shard_map/all_gather | solution.py:14
  228.8 2.0 collective-permute-start.5
Sparse Core Ops, SparseCore 0:
  13.2 63.8 all-gather.4
  106.9 61.2 all-gather.6
  197.2 28.6 all-gather.8
  242.2 26.4 all-gather.10
